TPU v7x, 32 devices: a whole 2x2x4 slice. The times are simulated.
32 devices in a mesh: blk: 8 (over z, y), chan: 4 (over x, core).
Axes of the slice: x: 2, y: 2, z: 4, core: 2. Of those that a mesh axis runs over, the one named last changes fastest.
Arguments:
- hidden_in: bfloat16 [2, 1, 2048, 768], P(None, None, ('blk', 'chan')), may hold values from -6 to 6
- cotangent: bfloat16 [2, 1, 2048, 768], P(None, None, ('blk', 'chan')), may hold values from -6 to 6
- mixer_input_weight: bfloat16 [768, 2304], P(None, ('blk', 'chan')), may hold values from -0.21875 to 0.21875
- mixer_output_weight: bfloat16 [768, 768], P(None, ('blk', 'chan')), may hold values from -0.21875 to 0.21875
- feedforward_up: bfloat16 [768, 3072], P(None, ('blk', 'chan')), may hold values from -0.21875 to 0.21875
- feedforward_down: bfloat16 [3072, 768], P(('blk', 'chan')), may hold values from -0.109375 to 0.109375
- first_gain: bfloat16 [768], P(('blk', 'chan')), may hold values from 0.5 to 1.5
- first_shift: bfloat16 [768], P(('blk', 'chan')), may hold values from -3 to 3
- second_gain: bfloat16 [768], P(('blk', 'chan')), may hold values from 0.5 to 1.5
- second_shift: bfloat16 [768], P(('blk', 'chan')), may hold values from -3 to 3
- short_taps: bfloat16 [3, 3, 768], P(None, None, ('blk', 'chan')), may hold values from -4 to 4
- short_bias: bfloat16 [3, 768], P(None, ('blk', 'chan')), may hold values from -3 to 3
- skip_scale: bfloat16 [768], P(('blk', 'chan')), may hold values from -4 to 4
- filter_out: bfloat16 [64, 768], P(None, ('blk', 'chan')), may hold values from -0.023925781 to 0.023925781
- pos_weight: bfloat16 [33, 64], replicated, may hold values from -1 to 1
- pos_bias: bfloat16 [64], replicated, may hold values from -4 to 4
- mid_weight: bfloat16 [64, 64], replicated, may hold values from -0.75 to 0.75
- mid_bias: bfloat16 [64], replicated, may hold values from -4 to 4
- sine_freq: bfloat16 [64], replicated, may hold values from 2 to 16
- decay_rate: bfloat16 [768], P(('blk', 'chan')), may hold values from 0.00024414062 to 0.029907227
Outputs:
- hidden_out: bfloat16 [2, 1, 2048, 768], P(None, None, ('blk', 'chan'))
- grad_hidden: bfloat16 [2, 1, 2048, 768], P(None, None, ('blk', 'chan'))
- grad_mixer_in: float32 [768, 2304], P(None, ('blk', 'chan'))
- grad_mixer_out: float32 [768, 768], P(None, ('blk', 'chan'))
- grad_mlp_up: float32 [768, 3072], P(None, ('blk', 'chan'))
- grad_mlp_down: float32 [3072, 768], P(('blk', 'chan'))
- grad_first_gain: float32 [768], P(('blk', 'chan'))
- grad_first_shift: float32 [768], P(('blk', 'chan'))
- grad_second_gain: float32 [768], P(('blk', 'chan'))
- grad_second_shift: float32 [768], P(('blk', 'chan'))
- grad_short_taps: float32 [3, 3, 768], P(None, None, ('blk', 'chan'))
- grad_short_bias: float32 [3, 768], P(None, ('blk', 'chan'))
- grad_skip_scale: float32 [768], P(('blk', 'chan'))
- grad_filter_out: float32 [64, 768], P(None, ('blk', 'chan'))
- grad_pos_weight: float32 [33, 64], replicated
- grad_pos_bias: float32 [64], replicated
- grad_mid_weight: float32 [64, 64], replicated
- grad_mid_bias: float32 [64], replicated
- grad_sine_freq: float32 [64], replicated
All inputs are finite; a program needn't handle non-finite values.
Results may differ from a plain program's by a relative error of at most 0.012.
Values may be sent and summed in bfloat16 or wider, within the bound.
A program may use at most 320 MiB of HBM per device.

v0:
```python
import math
import jax
import jax.numpy as jnp
from jax import lax
from jax.sharding import PartitionSpec as P

EPS = 1e-05
BANDS = 16
EXACT = lax.Precision.HIGHEST
AXES = ("blk", "chan")
F32 = jnp.float32
BF16 = jnp.bfloat16


def contract(a, b, dim_a, dim_b, precision=None):
    return lax.dot_general(
        a, b, (((dim_a,), (dim_b,)), ((), ())), precision=precision, preferred_element_type=F32
    )


def positions(length):
    lags = jnp.arange(length).astype(F32)
    band_freq = 0.0001 + (BANDS - 1 - 0.0001) * jnp.arange(BANDS).astype(F32) / (BANDS - 1)
    phase = 2.0 * math.pi / length * lags[None, :] * band_freq[:, None]
    return (
        lags,
        jnp.concatenate([lags[None, :] / (length - 1), jnp.cos(phase), -jnp.sin(phase)], 0),
    )


def filter_hidden(length, pos_weight, pos_bias, mid_weight, mid_bias, sine_freq):
    lags, features = positions(length)
    freq = sine_freq[:, None]
    first_sum = contract(pos_weight, features, 0, 0, EXACT) + pos_bias[:, None]
    first = jnp.sin(freq * first_sum)
    second_sum = contract(mid_weight, first, 0, 0, EXACT) + mid_bias[:, None]
    second = jnp.sin(freq * second_sum)
    return (lags, features, first_sum, first, second_sum, second)


def block_table(block):
    spot = lax.broadcasted_iota(jnp.int32, (block, block), 0)
    freq = lax.broadcasted_iota(jnp.int32, (block, block), 1)
    phase = math.pi / block * (spot * freq % (2 * block)).astype(F32)
    parity = 1.0 - 2.0 * (spot % 2).astype(F32)
    imag = jnp.where(freq == 0, parity, -jnp.sin(phase))
    return jnp.concatenate([jnp.cos(phase), imag], 1)


def to_spectrum(blocks, table):
    spec = lax.dot_general(
        blocks,
        table,
        (((blocks.ndim - 1,), (0,)), ((), ())),
        precision=EXACT,
        preferred_element_type=F32,
    )
    half = table.shape[0]
    return (spec[..., :half], spec[..., half:])


def from_spectrum(real, imag, table):
    half = table.shape[0]
    weight = jnp.where(lax.iota(jnp.int32, half) == 0, 0.5 / half, 1.0 / half)
    spec = jnp.concatenate([real * weight, imag * weight], -1)
    return lax.dot_general(
        spec,
        table,
        (((spec.ndim - 1,), (1,)), ((), ())),
        precision=EXACT,
        preferred_element_type=F32,
    )


def packed_kernel(real, imag):
    first = lax.iota(jnp.int32, real.shape[-1]) == 0
    return (real, jnp.where(first, imag, real), jnp.where(first, 0.0, imag))


def layer_norm(values, gain, shift):
    center = values - jnp.mean(values, -1, keepdims=True)
    scale_inv = lax.rsqrt(jnp.mean(center * center, -1, keepdims=True) + EPS)
    normal = center * scale_inv
    return (normal * gain + shift, normal, scale_inv)


def layer_norm_back(grad_out, normal, scale_inv, gain):
    grad_normal = grad_out * gain
    inner = grad_normal - jnp.mean(grad_normal, -1, keepdims=True)
    inner = inner - normal * jnp.mean(grad_normal * normal, -1, keepdims=True)
    return (inner * scale_inv, jnp.sum(grad_out * normal, 0), jnp.sum(grad_out, 0))


def gelu_parts(v):
    root = math.sqrt(2.0 / math.pi)
    inner = root * (v + 0.044715 * v * v * v)
    t = jnp.tanh(inner)
    value = 0.5 * v * (1.0 + t)
    slope = 0.5 * (1.0 + t) + 0.5 * v * (1.0 - t * t) * root * (1.0 + 3.0 * 0.044715 * v * v)
    return (value, slope)


def delayed(values, steps):
    if steps == 0:
        return values
    pad = jnp.zeros(values.shape[:-1] + (steps,), values.dtype)
    return jnp.concatenate([pad, values[..., :-steps]], -1)


def advanced(values, steps):
    if steps == 0:
        return values
    pad = jnp.zeros(values.shape[:-1] + (steps,), values.dtype)
    return jnp.concatenate([values[..., steps:], pad], -1)


def exchange(values):
    return lax.all_to_all(values, AXES, split_axis=0, concat_axis=0, tiled=True)


def shards(
    hidden_in,
    cotangent,
    mixer_input_weight,
    mixer_output_weight,
    feedforward_up,
    feedforward_down,
    first_gain,
    first_shift,
    second_gain,
    second_shift,
    short_taps,
    short_bias,
    skip_scale,
    filter_out,
    pos_weight,
    pos_bias,
    mid_weight,
    mid_bias,
    sine_freq,
    decay_rate,
):
    devices = lax.axis_size(AXES)
    micro, seq_count, tok, width = hidden_in.shape
    seqs = micro * seq_count
    tokens = seqs * tok
    length = tok * devices
    chans = width // devices
    block = tok * lax.axis_size("chan")
    blocks = length // block

    def gather(shard):
        return lax.all_gather(shard, AXES, axis=0, tiled=True)

    rows_in, rows_out, rows_up = (
        w.shape[1] for w in (mixer_input_weight, mixer_output_weight, feedforward_up)
    )
    weight_in = gather(mixer_input_weight.T)
    weight_out = gather(mixer_output_weight.T)
    weight_up = gather(feedforward_up.T)
    weight_down = gather(feedforward_down)
    norms = jnp.stack([first_gain, first_shift, second_gain, second_shift])
    norms = lax.all_gather(norms, AXES, axis=1, tiled=True).astype(F32)
    gain_one, shift_one, gain_two, shift_two = (norms[0], norms[1], norms[2], norms[3])
    freq = sine_freq.astype(F32)
    w_pos, w_mid, w_fil = (pos_weight.astype(F32), mid_weight.astype(F32), filter_out.astype(F32))
    lags, features, first_sum, first_act, second_sum, second_act = filter_hidden(
        length, w_pos, pos_bias.astype(F32), w_mid, mid_bias.astype(F32), freq
    )
    decay = jnp.exp(-lags[None, :] * decay_rate.astype(F32)[:, None])
    kernel = contract(w_fil, second_act, 0, 0, EXACT) * decay
    table = block_table(block)
    sign = 1.0 - 2.0 * (lax.iota(jnp.int32, block) % 2).astype(F32)
    ker_re, ker_im = to_spectrum(kernel.reshape(chans, blocks, block), table)

    def with_previous(spec):
        before = jnp.concatenate([jnp.zeros_like(spec[:, :1]), spec[:, :-1]], 1)
        return spec + sign * before

    k_re, k_alt, k_im = packed_kernel(with_previous(ker_re), with_previous(ker_im))
    values = hidden_in.reshape(tokens, width).astype(F32)
    normed, normal_one, inv_one = layer_norm(values, gain_one, shift_one)
    normed = normed.astype(BF16)
    projected = contract(weight_in, normed, 1, 1).astype(BF16)
    projected = projected.reshape(3, devices, chans, tokens).transpose(1, 0, 2, 3)
    arrived = exchange(projected)

    def by_sequence(values):
        parts = values.shape[1]
        values = values.reshape(devices, parts, chans, seqs, tok)
        return values.transpose(1, 3, 2, 0, 4).reshape(parts, seqs, chans, length)

    def by_device(values):
        parts = values.shape[0]
        values = values.reshape(parts, seqs, chans, devices, tok)
        return values.transpose(3, 0, 2, 1, 4).reshape(devices, parts, chans, tokens)

    steps = by_sequence(arrived).astype(F32)
    taps = short_taps.astype(F32)[:, :, None, :, None]
    conv = short_bias.astype(F32)[:, None, :, None]
    for i in range(3):
        conv = conv + taps[i] * delayed(steps, i)
    gate_out, gate_in, signal = (conv[0], conv[1], conv[2])
    gated = signal * gate_in
    sig_re, sig_im = to_spectrum(gated.reshape(seqs, chans, blocks, block), table)

    def shifted_sum(make):
        total = None
        for d in range(blocks):
            term = make(d)
            total = term if total is None else tuple((a + b for a, b in zip(total, term)))
        return total

    def ahead(x, d):
        return x if d == 0 else jnp.pad(x[:, :, :-d], ((0, 0), (0, 0), (d, 0), (0, 0)))

    def back(x, d):
        return x if d == 0 else jnp.pad(x[:, :, d:], ((0, 0), (0, 0), (0, d), (0, 0)))

    def forward_term(d):
        re, im = (ahead(sig_re, d), ahead(sig_im, d))
        kr, ka, ki = (k_re[:, d : d + 1], k_alt[:, d : d + 1], k_im[:, d : d + 1])
        return (re * kr - im * ki, re * ki + im * ka)

    out_re, out_im = shifted_sum(forward_term)
    long_out = from_spectrum(out_re, out_im, table).reshape(seqs, chans, length)
    skip = skip_scale.astype(F32)[None, :, None]
    long_total = long_out + skip * gated
    mixed = (long_total * gate_out).astype(BF16)
    mixed = exchange(by_device(mixed[None])).reshape(width, tokens)
    resid = values + contract(mixed, weight_out, 0, 1)
    second, normal_two, inv_two = layer_norm(resid, gain_two, shift_two)
    second = second.astype(BF16)
    upper = contract(second, weight_up, 1, 1)
    active, slope = gelu_parts(upper)
    active = active.astype(BF16)
    result = resid + contract(active, weight_down, 1, 0)
    cot = cotangent.reshape(tokens, width)
    grad_down = contract(active, cot, 0, 0)
    grad_upper = (contract(cot, weight_down, 1, 1) * slope).astype(BF16)
    grad_up = contract(grad_upper, second, 0, 0)
    grad_second = contract(grad_upper, weight_up, 1, 0)
    resid_term, grad_gain_two, grad_shift_two = layer_norm_back(
        grad_second, normal_two, inv_two, gain_two
    )
    grad_resid = cot.astype(F32) + resid_term
    grad_branch = grad_resid.astype(BF16)
    grad_out_w = contract(grad_branch, mixed, 0, 1)
    grad_mixed = contract(weight_out, grad_branch, 0, 1).astype(BF16)
    grad_mixed = exchange(grad_mixed.reshape(devices, 1, chans, tokens))
    grad_mixed = by_sequence(grad_mixed)[0].astype(F32)
    grad_gate_out = grad_mixed * long_total
    grad_long = grad_mixed * gate_out
    grad_skip = jnp.sum(grad_long * gated, (0, 2))
    gl_re, gl_im = to_spectrum(grad_long.reshape(seqs, chans, blocks, block), table)

    def signal_term(d):
        re, im = (back(gl_re, d), back(gl_im, d))
        kr, ka, ki = (k_re[:, d : d + 1], k_alt[:, d : d + 1], k_im[:, d : d + 1])
        return (re * kr + im * ki, im * ka - re * ki)

    gg_re, gg_im = shifted_sum(signal_term)
    grad_gated = from_spectrum(gg_re, gg_im, table).reshape(seqs, chans, length) + skip * grad_long
    first_slot = lax.iota(jnp.int32, block) == 0
    kg_re, kg_im = ([], [])
    for d in range(blocks):
        s_re, s_im = (sig_re[:, :, : blocks - d], sig_im[:, :, : blocks - d])
        g_re, g_im = (gl_re[:, :, d:], gl_im[:, :, d:])
        same, other = (g_re * s_re, g_im * s_im)
        kg_re.append(jnp.sum(jnp.where(first_slot, same, same + other), (0, 2)))
        kg_im.append(jnp.sum(jnp.where(first_slot, other, g_im * s_re - g_re * s_im), (0, 2)))
    kg_re, kg_im = (jnp.stack(kg_re, 1), jnp.stack(kg_im, 1))

    def with_next(spec):
        after = jnp.concatenate([spec[:, 1:], jnp.zeros_like(spec[:, :1])], 1)
        return spec + sign * after

    grad_kernel = from_spectrum(with_next(kg_re), with_next(kg_im), table).reshape(chans, length)
    grad_conv = jnp.stack([grad_gate_out, grad_gated * signal, grad_gated * gate_in])
    grad_bias = jnp.sum(grad_conv, (1, 3))
    grad_taps = jnp.stack([jnp.sum(grad_conv * delayed(steps, i), (1, 3)) for i in range(3)])
    grad_steps = taps[0] * grad_conv
    for i in (1, 2):
        grad_steps = grad_steps + taps[i] * advanced(grad_conv, i)
    grad_proj = exchange(by_device(grad_steps.astype(BF16)))
    grad_proj = grad_proj.transpose(1, 0, 2, 3).reshape(3 * width, tokens)
    fade = grad_kernel * decay
    grad_filter = contract(second_act, fade, 1, 1, EXACT)
    grad_two = contract(w_fil, fade, 1, 0, EXACT) * jnp.cos(freq[:, None] * second_sum)
    grad_freq = jnp.sum(grad_two * second_sum, 1)
    grad_two = grad_two * freq[:, None]
    grad_mid = contract(first_act, grad_two, 1, 1, EXACT)
    grad_one = contract(w_mid, grad_two, 1, 0, EXACT) * jnp.cos(freq[:, None] * first_sum)
    grad_freq = grad_freq + jnp.sum(grad_one * first_sum, 1)
    grad_one = grad_one * freq[:, None]
    grad_pos = contract(features, grad_one, 1, 1, EXACT)
    small = lax.psum(
        jnp.concatenate(
            [
                grad_pos,
                jnp.sum(grad_one, 1)[None],
                grad_mid,
                jnp.sum(grad_two, 1)[None],
                grad_freq[None],
            ]
        ),
        AXES,
    )
    emb, order = pos_weight.shape
    grad_in = contract(grad_proj, normed, 1, 0)
    grad_normed = contract(grad_proj, weight_in, 0, 0)
    input_term, grad_gain_one, grad_shift_one = layer_norm_back(
        grad_normed, normal_one, inv_one, gain_one
    )
    grad_hidden = (grad_resid + input_term).astype(BF16)

    def reduce_rows(partial):
        return lax.psum_scatter(partial.astype(BF16), AXES, scatter_dimension=0, tiled=True).astype(
            F32
        )

    norm_grads = jnp.stack([grad_gain_one, grad_shift_one, grad_gain_two, grad_shift_two])
    norm_grads = lax.psum_scatter(norm_grads, AXES, scatter_dimension=1, tiled=True)
    return (
        result.astype(BF16).reshape(hidden_in.shape),
        grad_hidden.reshape(hidden_in.shape),
        reduce_rows(grad_in).T,
        reduce_rows(grad_out_w).T,
        reduce_rows(grad_up).T,
        reduce_rows(grad_down),
        norm_grads[0],
        norm_grads[1],
        norm_grads[2],
        norm_grads[3],
        grad_taps,
        grad_bias,
        grad_skip,
        grad_filter,
        small[:emb],
        small[emb],
        small[emb + 1 : emb + 1 + order],
        small[emb + 1 + order],
        small[emb + 2 + order],
    )


def solution(mesh):
    rows, spread, tokens = (P(AXES), P(None, AXES), P(None, None, AXES, None))
    params = (
        rows,
        rows,
        rows,
        rows,
        P(None, None, AXES),
        spread,
        rows,
        spread,
        P(),
        P(),
        P(),
        P(),
        P(),
    )
    return jax.shard_map(
        shards,
        mesh=mesh,
        in_specs=(tokens, tokens, spread, spread, spread, P(AXES, None)) + params + (rows,),
        out_specs=(tokens, tokens, spread, spread, spread, P(AXES, None)) + params,
        check_vma=False,
    )
```

profile of v0, /device:TPU:0, one launch (start us, length us, event | category | flops | bytes accessed | tf_op | source)
XLA Modules:
  0.0 719.1 jit_solution(14635279991504066053)
XLA Ops:
  13.0 43.4 %all-gather = bf16[32,24,4]{1,2,0:T(4,128)(2,1)S(1)} all-gather(bf16[1,24,4]{1,2,0:T(4,128)(2,1)S(1)} %maximum_bitcast_fusion), channel_id=1, replica_groups=mesh['blk'=8,'chan'=4] {'blk','chan'}, dimensions={0}, use_global_device_ids=true | all-gather | bytes 6336 | tf_op jit(solution)/shard_map/all_gather | solution.py:163
  62.6 2.2 fusion.6
  64.8 2.1 fusion.7
  71.0 2.8 all-gather.6.cloned.1.call-done
  73.7 3.3 fusion.1
  78.2 3.7 all-to-all-start
  96.5 3.0 all-to-all-done
  99.5 2.6 reshape.386
  102.1 1.4 copy-done.1
  103.5 2.1 copy.121
  105.6 2.2 reshape.381
  118.6 1.8 fusion.79
  121.6 1.9 reshape.368
  123.5 3.8 all-to-all-start.1
  127.3 3.1 all-gather.8.cloned.1.call-done
  130.4 5.8 all-to-all-done.1
  136.2 2.0 fusion.136
  138.4 57.5 %all-gather.10.cloned.1.call-done = bf16[3072,768]{1,0:T(8,128)(2,1)} async-done(((bf16[96,768]{1,0:T(8,128)(2,1)}), bf16[3072,768]{1,0:T(8,128)(2,1)}) %all-gather.10.cloned.1.call-update) | async-done | bytes 4718608 | tf_op jit(solution)/shard_map/all_gather | solution.py:153
  195.9 5.3 fusion.123
  201.2 60.0 %all-gather.12.cloned.1.call-done = bf16[3072,768]{1,0:T(8,128)(2,1)} async-done(((bf16[96,768]{1,0:T(8,128)(2,1)}), bf16[3072,768]{1,0:T(8,128)(2,1)}) %all-gather.12.cloned.1.call-update) | async-done | bytes 4718608 | tf_op jit(solution)/shard_map/all_gather | solution.py:153
  261.1 4.8 fusion
  265.9 1.5 multiply_reduce_fusion.6
  269.7 1.7 copy.124
  271.4 3.5 all-to-all-start.2
  275.0 1.8 reshape.373
  277.7 2.5 convolution_convert_fusion.4
  280.2 3.6 all-to-all-done.2
  283.9 2.3 reshape.387
  286.2 1.4 copy.126
  288.6 2.0 fusion.24
  297.2 1.4 fusion.64
  298.6 1.4 fusion.58
  300.0 2.2 reshape.382
  302.2 2.8 fusion.19
  304.9 1.8 reshape.374
  306.7 1.8 slice_multiply_fusion.2
  311.1 2.3 fusion.124
  313.4 2.3 reshape.375
  315.7 2.2 copy.128
  318.0 3.3 reshape.376
  321.3 2.7 all-to-all-start.3
  325.0 18.6 %all-to-all-done.3 = bf16[32,3,24,128]{3,2,1,0:T(8,128)(2,1)S(1)} async-done(((bf16[32,3,24,128]{3,2,1,0:T(8,128)(2,1)}), bf16[32,3,24,128]{3,2,1,0:T(8,128)(2,1)S(1)}, u32[]{:S(2)}, u32[]{:S(2)}) %all-to-all-start.3) | async-done | bytes 589856 | tf_op jit(solution)/shard_map/all_to_all | solution.py:118
  343.6 4.0 convolution_convert_fusion.2
  348.8 3.7 convolution_convert_fusion.1
  353.4 5.3 convolution_convert_fusion
  359.4 4.6 fusion.13
  365.3 2.3 stack.126
  372.9 2.0 fusion.5
  375.0 3.5 multiply_reduce_fusion.3
  378.8 1.6 copy.132
  380.4 1.6 copy.131
  382.0 1.5 copy.130
  384.2 2.3 fusion.35
  386.7 3.8 fusion.2
  391.2 1.7 fusion.84
  392.9 2.9 fusion.36
  396.8 39.7 %all-reduce.37 = (f32[4,768]{1,0:T(4,128)S(1)}, f32[100,64]{0,1:T(8,128)S(1)}) all-reduce(f32[4,768]{1,0:T(4,128)S(1)} %pad_maximum_fusion.11, f32[100,64]{0,1:T(8,128)S(1)} %concatenate.60), channel_id=6, replica_groups=mesh['blk'=8,'chan'=4] {'blk','chan'}, use_global_device_ids=true, to_apply=%region_16.17.clone | all-reduce | flops 9472 | bytes 75776
  440.2 1.4 convert_bitcast_fusion.2
  441.6 44.7 %reduce-scatter.6.cloned.1.call-done = bf16[72,768]{1,0:T(8,128)(2,1)} async-done(((bf16[2304,768]{1,0:T(8,128)(2,1)}), bf16[72,768]{1,0:T(8,128)(2,1)}) %reduce-scatter.6.cloned.1.call-update) | async-done | bytes 110608 | tf_op jit(solution)/shard_map/reduce_scatter | solution.py:318
  486.3 1.6 convert_bitcast_fusion.1
  487.9 109.8 %reduce-scatter.10.cloned.1.call-done = bf16[96,768]{1,0:T(8,128)(2,1)} async-done(((bf16[3072,768]{1,0:T(8,128)(2,1)}), bf16[96,768]{1,0:T(8,128)(2,1)}) %reduce-scatter.10.cloned.1.call-update) | async-done | bytes 147472 | tf_op jit(solution)/shard_map/reduce_scatter | solution.py:318
  597.7 1.6 convert_bitcast_fusion
  599.3 110.9 %reduce-scatter.12.cloned.1.call-done = bf16[96,768]{1,0:T(8,128)(2,1)} async-done(((bf16[3072,768]{1,0:T(8,128)(2,1)}), bf16[96,768]{1,0:T(8,128)(2,1)}) %reduce-scatter.12.cloned.1.call-update) | async-done | bytes 147472 | tf_op jit(solution)/shard_map/reduce_scatter | solution.py:318
  710.2 1.6 convert_element_type.304
  (469 shorter events, 72.3 us)
Async XLA Ops:
  7.2 55.4 %copy-start = (bf16[64,64]{1,0:T(8,128)(2,1)S(1)}, bf16[64,64]{1,0:T(8,128)(2,1)}, u32[]{:S(2)}) copy-start(bf16[64,64]{1,0:T(8,128)(2,1)} %param.36) | copy-start | bytes 24580
  7.2 66.5 %all-gather.6.cloned.1.call-start = ((), (), s32[]{:S(2)}) async-start(), calls=%async_computation.8 | async-start | bytes 3649536 | tf_op jit(solution)/shard_map/all_gather | solution.py:153
  7.9 122.4 %all-gather.8.cloned.1.call-start = ((), (), s32[]{:S(2)}) async-start(), calls=%async_computation.9 | async-start | bytes 1216512 | tf_op jit(solution)/shard_map/all_gather | solution.py:153
  8.7 187.2 %all-gather.10.cloned.1.call-start = ((), (), s32[]{:S(2)}) async-start(), calls=%async_computation.10 | async-start | bytes 4866048 | tf_op jit(solution)/shard_map/all_gather | solution.py:153
  8.7 56.0 %copy-start.119 = (bf16[64,24]{0,1:T(8,128)(2,1)S(1)}, bf16[64,24]{0,1:T(8,128)(2,1)}, u32[]{:S(2)}) copy-start(bf16[64,24]{0,1:T(8,128)(2,1)} %param.33) | copy-start | bytes 9220
  9.4 251.7 %all-gather.12.cloned.1.call-start = ((), (), s32[]{:S(2)}) async-start(), calls=%async_computation.11 | async-start | bytes 4866048 | tf_op jit(solution)/shard_map/all_gather | solution.py:153
  12.3 57.9 %copy-start.139 = (f32[128]{0:T(128)}, f32[128]{0:T(128)S(1)}, u32[]{:S(2)}) copy-start(f32[128]{0:T(128)S(1)} %div.40) | copy-start | bytes 1540
  12.3 54.6 %copy-start.106 = (f32[1,2048]{1,0:T(1,128)}, f32[1,2048]{1,0:T(1,128)S(1)}, u32[]{:S(2)}) copy-start(f32[1,2048]{1,0:T(1,128)S(1)} %convert_multiply_fusion.1) | copy-start | bytes 24580
  56.8 13.4 %copy-start.141 = (f32[128]{0:T(128)}, f32[128]{0:T(128)S(1)}, u32[]{:S(2)}) copy-start(f32[128]{0:T(128)S(1)} %rsqrt.21) | copy-start | bytes 1540
  60.2 6.8 copy-start.117
  60.8 6.1 copy-start.143
  61.4 6.2 copy-start.41
  61.4 6.2 copy-start.43
  62.6 7.8 %copy-start.17 = (f32[64,2048]{1,0:T(8,128)}, f32[64,2048]{1,0:T(8,128)S(1)}, u32[]{:S(2)}) copy-start(f32[64,2048]{1,0:T(8,128)S(1)} %fusion.3) | copy-start | bytes 1572868
  62.6 7.7 %copy-start.14 = (bf16[2,1,64,768]{3,2,1,0:T(8,128)(2,1)S(1)}, bf16[2,1,64,768]{3,2,1,0:T(8,128)(2,1)}, u32[]{:S(2)}) copy-start(bf16[2,1,64,768]{3,2,1,0:T(8,128)(2,1)} %param.20) | copy-start | bytes 589828
  64.8 6.2 copy-start.5
  67.0 15.0 %copy-start.108 = (pred[256]{0:T(512)(128)(4,1)}, pred[256]{0:T(512)(128)(4,1)S(1)}, u32[]{:S(2)}) copy-start(pred[256]{0:T(512)(128)(4,1)S(1)} %get-tuple-element.236) | copy-start | bytes 772
  67.6 14.4 %copy-start.133 = (f32[256]{0:T(256)}, f32[256]{0:T(256)S(1)}, u32[]{:S(2)}) copy-start(f32[256]{0:T(256)S(1)} %get-tuple-element.239) | copy-start | bytes 3076
  68.2 8.8 %copy-start.111 = (f32[768]{0:T(1024)}, f32[768]{0:T(1024)S(1)}, u32[]{:S(2)}) copy-start(f32[768]{0:T(1024)S(1)} %get-tuple-element.150) | copy-start | bytes 9220
  70.2 46.5 %copy-start.8 = (f32[256,256]{1,0:T(8,128)}, f32[256,256]{1,0:T(8,128)S(1)}, u32[]{:S(2)}) copy-start(f32[256,256]{1,0:T(8,128)S(1)} %negate_select_fusion.2) | copy-start | bytes 786436
  78.2 21.3 %all-to-all-start = ((bf16[32,3,24,128]{3,2,1,0:T(8,128)(2,1)}), bf16[32,3,24,128]{3,2,1,0:T(8,128)(2,1)}, u32[]{:S(2)}, u32[]{:S(2)}) async-start(bf16[32,3,24,128]{3,2,1,0:T(8,128)(2,1)} %copy.120), calls=%async_computation | async-start | bytes 1179648 | tf_op jit(solution)/shard_map/all_to_all | solution.py:118
  82.0 13.9 %copy-start.149 = (bf16[24]{0:T(256)(128)(2,1)S(1)}, bf16[24]{0:T(256)(128)(2,1)}, u32[]{:S(2)}) copy-start(bf16[24]{0:T(256)(128)(2,1)} %param.32) | copy-start | bytes 148
  96.5 11.3 %copy-start.121 = (f32[3,24]{1,0:T(4,128)}, f32[3,24]{1,0:T(4,128)S(1)}, u32[]{:S(2)}) copy-start(f32[3,24]{1,0:T(4,128)S(1)} %get-tuple-element.219) | copy-start | bytes 868
  96.5 11.4 %copy-start.123 = (f32[3,24]{1,0:T(4,128)}, f32[3,24]{1,0:T(4,128)S(1)}, u32[]{:S(2)}) copy-start(f32[3,24]{1,0:T(4,128)S(1)} %get-tuple-element.220) | copy-start | bytes 868
  96.5 11.4 %copy-start.125 = (f32[3,24]{1,0:T(4,128)}, f32[3,24]{1,0:T(4,128)S(1)}, u32[]{:S(2)}) copy-start(f32[3,24]{1,0:T(4,128)S(1)} %get-tuple-element.221) | copy-start | bytes 868
  123.5 12.7 %all-to-all-start.1 = ((bf16[32,1,24,128]{3,2,1,0:T(8,128)(2,1)}), bf16[32,1,24,128]{3,2,1,0:T(8,128)(2,1)S(1)}, u32[]{:S(2)}, u32[]{:S(2)}) async-start(bf16[32,1,24,128]{3,2,1,0:T(8,128)(2,1)} %bitcast.23), calls=%async_computation.1 | async-start | bytes 393216 | tf_op jit(solution)/shard_map/all_to_all | solution.py:118
  136.2 65.0 %copy-start.39 = (bf16[32,1,24,128]{3,2,1,0:T(8,128)(2,1)}, bf16[32,1,24,128]{3,2,1,0:T(8,128)(2,1)S(1)}, u32[]{:S(2)}) copy-start(bf16[32,1,24,128]{3,2,1,0:T(8,128)(2,1)S(1)} %all-to-all-done.1) | copy-start | bytes 589828
  138.2 129.3 %copy-start.129 = (f32[128]{0:T(128)}, f32[128]{0:T(128)S(1)}, u32[]{:S(2)}) copy-start(f32[128]{0:T(128)S(1)} %broadcast_multiply_fusion.5) | copy-start | bytes 1540
  138.4 129.1 %copy-start.135 = (f32[128]{0:T(128)}, f32[128]{0:T(128)S(1)}, u32[]{:S(2)}) copy-start(f32[128]{0:T(128)S(1)} %add_rsqrt_fusion.1) | copy-start | bytes 1540
  195.9 65.2 %copy-start.45 = (bf16[2,1,64,768]{3,2,1,0:T(8,128)(2,1)S(1)}, bf16[2,1,64,768]{3,2,1,0:T(8,128)(2,1)}, u32[]{:S(2)}) copy-start(bf16[2,1,64,768]{3,2,1,0:T(8,128)(2,1)} %param.21) | copy-start | bytes 589828
  261.1 4.8 copy-start.3
  268.7 9.1 %copy-start.22 = (f32[128,768]{1,0:T(8,128)}, f32[128,768]{1,0:T(8,128)S(1)}, u32[]{:S(2)}) copy-start(f32[128,768]{1,0:T(8,128)S(1)} %multiply_add_fusion.3) | copy-start | bytes 1179652
  271.4 12.4 %all-to-all-start.2 = ((bf16[32,1,24,128]{3,2,1,0:T(8,128)(2,1)}), bf16[32,1,24,128]{3,2,1,0:T(8,128)(2,1)}, u32[]{:S(2)}, u32[]{:S(2)}) async-start(bf16[32,1,24,128]{3,2,1,0:T(8,128)(2,1)} %bitcast.300), calls=%async_computation.2 | async-start | bytes 393216 | tf_op jit(solution)/shard_map/all_to_all | solution.py:118
  275.0 165.2 %reduce-scatter.8.cloned.1.call-start = ((), (), s32[]{:S(2)}) async-start(), calls=%async_computation.13 | async-start | bytes 1216512 | tf_op jit(solution)/shard_map/reduce_scatter | solution.py:318
  300.0 6.8 copy-start.148
  318.0 6.1 copy-start.15
  318.0 6.1 copy-start.112
  318.0 6.1 copy-start.132
  318.0 6.1 copy-start.147
  321.3 22.2 %all-to-all-start.3 = ((bf16[32,3,24,128]{3,2,1,0:T(8,128)(2,1)}), bf16[32,3,24,128]{3,2,1,0:T(8,128)(2,1)S(1)}, u32[]{:S(2)}, u32[]{:S(2)}) async-start(bf16[32,3,24,128]{3,2,1,0:T(8,128)(2,1)} %reshape.376), calls=%async_computation.3 | async-start | bytes 1179648 | tf_op jit(solution)/shard_map/all_to_all | solution.py:118
  324.0 162.2 %reduce-scatter.6.cloned.1.call-start = ((), (), s32[]{:S(2)}) async-start(), calls=%async_computation.12 | async-start | bytes 3649536 | tf_op jit(solution)/shard_map/reduce_scatter | solution.py:318
  343.6 4.1 copy-start.29
  347.7 250.0 %reduce-scatter.10.cloned.1.call-start = ((), (), s32[]{:S(2)}) async-start(), calls=%async_computation.14 | async-start | bytes 4866048 | tf_op jit(solution)/shard_map/reduce_scatter | solution.py:318
  352.5 357.6 %reduce-scatter.12.cloned.1.call-start = ((), (), s32[]{:S(2)}) async-start(), calls=%async_computation.15 | async-start | bytes 4866048 | tf_op jit(solution)/shard_map/reduce_scatter | solution.py:318
  359.4 4.6 copy-start.25
  364.0 3.6 copy-start.27
  364.0 4.9 copy-start.11
  365.3 4.6 copy-start.110
  372.9 5.8 copy-start.35
  375.0 5.4 copy-start.36
  380.4 3.8 copy-start.19
  380.4 3.8 copy-start.33
  382.0 4.6 copy-start.2
  386.7 3.9 copy-start.137
  386.7 3.9 copy-start.138
  386.7 4.5 copy-start.13
  386.7 4.5 copy-start.40
  386.7 6.3 copy-start.145
  386.7 9.1 %copy-start.4 = (bf16[2304,768]{1,0:T(8,128)(2,1)S(1)}, bf16[2304,768]{1,0:T(8,128)(2,1)}, u32[]{:S(2)}) copy-start(bf16[2304,768]{1,0:T(8,128)(2,1)} %all-gather.6.cloned.1.call-done) | copy-start | bytes 10616836
  390.6 5.3 copy-start.16
  390.6 5.3 copy-start.30
  390.6 5.3 copy-start.140
  390.6 5.3 copy-start.142
  395.9 43.4 %copy-start.23 = (f32[128,768]{1,0:T(8,128)S(1)}, f32[128,768]{1,0:T(8,128)}, u32[]{:S(2)}) copy-start(f32[128,768]{1,0:T(8,128)} %copy-done.22) | copy-start | bytes 1179652
  (98 other events, 133.0 us)
Sparse Core Ops, SparseCore 0:
  10.9 62.7 all-gather.5
  76.6 53.7 all-gather.7
  133.3 62.5 all-gather.9
  198.7 62.4 all-gather.11
  280.6 98.2 reduce-scatter.7
  384.1 102.0 reduce-scatter.5
  491.7 105.8 reduce-scatter.9
  604.0 106.0 reduce-scatter.11
where the time goes:
time: 728 us; the launch traced here: 719 us
  waiting for transfers between devices  422 us (58%)
  blocking collectives  83.1 us (11%)
  local copies, waits for them, and re-layouts  74.8 us (10%)
  matrix products  63.1 us (9%)
  other arithmetic  44.8 us (6%)
  between operations  16.8 us (2%)
  starting transfers between devices  14.3 us (2%)
    reduce_scatter x4, waiting for transfers between devices, reduce_rows(): lax.psum_scatter(partial.astype(BF16), AXES, scatter_dimension=0, tiled=T...  265 us
    all_gather x4, waiting for transfers between devices, gather(): return lax.all_gather(shard, AXES, axis=0, tiled=True)  123 us
    dot_general x20, matrix products, contract(): lax.dot_general(a, b, (((dim_a,), (dim_b,)), ((), ())), precision=precisi...  55.4 us
    all_gather x1, blocking collectives, shards(): norms = lax.all_gather(norms, AXES, axis=1, tiled=True).astype(F32)  43.4 us
    unnamed x1, blocking collectives  39.7 us
    all_to_all x4, waiting for transfers between devices, exchange(): return lax.all_to_all(values, AXES, split_axis=0, concat_axis=0, tiled=True)  31 us
    unnamed x331, local copies, waits for them, and re-layouts  23.3 us
  transfers between devices with their start and end apart: 12, of which 11 were waited for; matrix products, arithmetic and copies ran while one was open for 23% of the time, Pallas kernels for 0%

commit v1 on v0

--- a/solution.py
+++ b/solution.py
@@ -10,6 +10,31 @@
 AXES = ("blk", "chan")
 F32 = jnp.float32
 BF16 = jnp.bfloat16
+
+
+def launch_the_shelves(buf, row_dim):
+    buf = jnp.moveaxis(buf, 0, row_dim)
+    v1 = buf.shape
+    return buf.reshape(*v1[:row_dim], v1[row_dim] * v1[row_dim + 1], *v1[row_dim + 2 :])
+
+
+def _match_loads(z_in, across):
+    a_next = lax.psum(1, axis_name=across)
+    b_next = lax.axis_index(across)
+    z1, base_arr = (a_next, b_next)
+    z, block_next = (z_in[None], 1)
+    while block_next < z1:
+        p_next = lax.ppermute(z, axis_name=across, perm=[(u, u ^ block_next) for u in range(z1)])
+        wide_out = base_arr & block_next == 0
+        current_value = jnp.where(wide_out, z, p_next)
+        z = jnp.concatenate([current_value, jnp.where(wide_out, p_next, z)])
+        block_next *= 2
+    return z
+
+
+def draw_keys_over_axis(load, xs, k_dim):
+    y_new = _match_loads(load, xs)
+    return launch_the_shelves(y_new, k_dim)
 
 
 def contract(a, b, dim_a, dim_b, precision=None):
@@ -150,7 +175,7 @@
     blocks = length // block
 
     def gather(shard):
-        return lax.all_gather(shard, AXES, axis=0, tiled=True)
+        return draw_keys_over_axis(shard, AXES, 0)
 
     rows_in, rows_out, rows_up = (
         w.shape[1] for w in (mixer_input_weight, mixer_output_weight, feedforward_up)

time: 728 us -> 916 us (1.26)
  waiting for transfers between devices: 422 us -> 554 us
  other arithmetic: 44.8 us -> 66.9 us
  blocking collectives: 83.1 us -> 105 us
  starting transfers between devices: 14.3 us -> 26.9 us
    ppermute x0 -> x20, waiting for transfers between devices: none -> 188 us  [_match_loads(): lax.ppermute(z, axis_name=across, perm=[(u, u ^ block_next) for u in rang...]
    all_gather x4 -> x0, waiting for transfers between devices: 123 us -> none  [gather(): return lax.all_gather(shard, AXES, axis=0, tiled=True)]
    all_to_all x4 -> x3, waiting for transfers between devices: 31 us -> 99.2 us  [exchange(): return lax.all_to_all(values, AXES, split_axis=0, concat_axis=0, tiled=True)]
    all_to_all x0 -> x1, blocking collectives: none -> 21.9 us  [exchange(): return lax.all_to_all(values, AXES, split_axis=0, concat_axis=0, tiled=True)]
    ppermute x0 -> x20, starting transfers between devices: none -> 14 us  [_match_loads(): lax.ppermute(z, axis_name=across, perm=[(u, u ^ block_next) for u in rang...]
    concatenate x0 -> x20, other arithmetic: none -> 14 us  [_match_loads(): z = jnp.concatenate([current_value, jnp.where(wide_out, p_next, z)])]
    select_n x0 -> x19, other arithmetic: none -> 9.21 us  [_match_loads(): current_value = jnp.where(wide_out, z, p_next)]
    unnamed x331 -> x377, local copies, waits for them, and re-layouts: 23.3 us -> 26.4 us
  transfers between devices with their start and end apart: 12 -> 27, of which waited for: 11 -> 16; matrix products, arithmetic and copies ran while one was open for 23% -> 20% of each run, Pallas kernels for 0% -> 0%
where the time goes in v1:
time: 916 us; the launch traced here: 905 us
  waiting for transfers between devices  554 us (60%)
  blocking collectives  105 us (11%)
  local copies, waits for them, and re-layouts  78.9 us (9%)
  other arithmetic  66.9 us (7%)
  matrix products  56.1 us (6%)
  starting transfers between devices  26.9 us (3%)
  between operations  17.1 us (2%)
    reduce_scatter x4, waiting for transfers between devices, reduce_rows(): lax.psum_scatter(partial.astype(BF16), AXES, scatter_dimension=0, tiled=T...  267 us
    ppermute x20, waiting for transfers between devices, _match_loads(): lax.ppermute(z, axis_name=across, perm=[(u, u ^ block_next) for u in rang...  188 us
    all_to_all x3, waiting for transfers between devices, exchange(): return lax.all_to_all(values, AXES, split_axis=0, concat_axis=0, tiled=True)  99.2 us
    dot_general x20, matrix products, contract(): lax.dot_general(a, b, (((dim_a,), (dim_b,)), ((), ())), precision=precisi...  48.5 us
    all_gather x1, blocking collectives, shards(): norms = lax.all_gather(norms, AXES, axis=1, tiled=True).astype(F32)  43.2 us
    unnamed x1, blocking collectives  39.5 us
    unnamed x377, local copies, waits for them, and re-layouts  26.4 us
    all_to_all x1, blocking collectives, exchange(): return lax.all_to_all(values, AXES, split_axis=0, concat_axis=0, tiled=True)  21.9 us
  transfers between devices with their start and end apart: 27, of which 16 were waited for; matrix products, arithmetic and copies ran while one was open for 20% of the time, Pallas kernels for 0%

profile of v1, /device:TPU:0, one launch (start us, length us, event | category | flops | bytes accessed | tf_op | source)
XLA Modules:
  0.0 904.6 jit_solution(3252164599136780005)
XLA Ops:
  10.7 43.2 %all-gather = bf16[32,24,4]{1,2,0:T(4,128)(2,1)S(1)} all-gather(bf16[1,24,4]{1,2,0:T(4,128)(2,1)S(1)} %maximum_bitcast_fusion), channel_id=1, replica_groups=mesh['blk'=8,'chan'=4] {'blk','chan'}, dimensions={0}, use_global_device_ids=true | all-gather | bytes 6336 | tf_op jit(solution)/shard_map/all_gather | solution.py:188
  62.1 2.2 fusion.6
  64.2 2.1 fusion.7
  70.2 2.1 collective-permute-start.6
  72.2 6.1 collective-permute-done.1
  94.0 2.1 collective-permute-start.7
  96.3 2.1 collective-permute-start.11
  99.3 2.1 collective-permute-start.8
  101.3 15.5 %collective-permute-done.3 = bf16[8,72,768]{2,1,0:T(8,128)(2,1)S(1)} collective-permute-done((bf16[8,72,768]{2,1,0:T(8,128)(2,1)S(1)}, bf16[8,72,768]{2,1,0:T(8,128)(2,1)S(1)}, u32[]{:S(2)}, u32[]{:S(2)}) %collective-permute-start.3) | collective-permute-done | bytes 884768 | tf_op jit(solution)/shard_map/ppermute | solution.py:27
  117.4 2.0 collective-permute-start.17
  119.6 2.5 collective-permute-done.8
  124.6 9.1 %collective-permute-done.17 = bf16[4,96,768]{2,1,0:T(8,128)(2,1)S(1)} collective-permute-done((bf16[4,96,768]{2,1,0:T(8,128)(2,1)S(1)}, bf16[4,96,768]{2,1,0:T(8,128)(2,1)S(1)}, u32[]{:S(2)}, u32[]{:S(2)}) %collective-permute-start.17) | collective-permute-done | bytes 589856 | tf_op jit(solution)/shard_map/ppermute | solution.py:27
  134.9 5.9 collective-permute-done.12
  142.6 63.7 %collective-permute-done.4 = bf16[16,72,768]{2,1,0:T(8,128)(2,1)S(1)} collective-permute-done((bf16[16,72,768]{2,1,0:T(8,128)(2,1)S(1)}, bf16[16,72,768]{2,1,0:T(8,128)(2,1)S(1)}, u32[]{:S(2)}, u32[]{:S(2)}) %collective-permute-start.4) | collective-permute-done | bytes 1769504 | tf_op jit(solution)/shard_map/ppermute | solution.py:27
  209.7 4.9 all-to-all-start
  214.6 3.0 collective-permute-done.9
  221.3 1.8 pad_maximum_fusion.4
  223.6 9.6 %collective-permute-done.13 = bf16[8,96,768]{2,1,0:T(8,128)(2,1)} collective-permute-done((bf16[8,96,768]{2,1,0:T(8,128)(2,1)}, bf16[8,96,768]{2,1,0:T(8,128)(2,1)}, u32[]{:S(2)}, u32[]{:S(2)}) %collective-permute-start.13) | collective-permute-done | bytes 1179680 | tf_op jit(solution)/shard_map/ppermute | solution.py:27
  234.6 1.8 pad_maximum_fusion.3
  236.7 95.8 %all-to-all-done = bf16[32,3,24,128]{3,2,1,0:T(8,128)(2,1)} async-done(((bf16[32,3,24,128]{3,2,1,0:T(8,128)(2,1)}), bf16[32,3,24,128]{3,2,1,0:T(8,128)(2,1)}, u32[]{:S(2)}, u32[]{:S(2)}) %all-to-all-start) | async-done | bytes 589856 | tf_op jit(solution)/shard_map/all_to_all | solution.py:143
  332.6 2.6 reshape.427
  336.7 2.2 copy.111
  338.9 2.2 reshape.422
  356.2 1.9 reshape.406
  358.1 3.7 all-to-all-start.1
  361.9 23.4 %collective-permute-done.19 = bf16[16,96,768]{2,1,0:T(8,128)(2,1)} collective-permute-done((bf16[16,96,768]{2,1,0:T(8,128)(2,1)}, bf16[16,96,768]{2,1,0:T(8,128)(2,1)}, u32[]{:S(2)}, u32[]{:S(2)}) %collective-permute-start.19) | collective-permute-done | bytes 2359328 | tf_op jit(solution)/shard_map/ppermute | solution.py:27
  385.3 2.3 broadcast_select_fusion.1
  387.6 48.2 %collective-permute-done.14 = bf16[16,96,768]{2,1,0:T(8,128)(2,1)} collective-permute-done((bf16[16,96,768]{2,1,0:T(8,128)(2,1)}, bf16[16,96,768]{2,1,0:T(8,128)(2,1)}, u32[]{:S(2)}, u32[]{:S(2)}) %collective-permute-start.14) | collective-permute-done | bytes 2359328 | tf_op jit(solution)/shard_map/ppermute | solution.py:27
  435.8 2.0 broadcast_select_fusion.3
  437.8 2.6 pad_maximum_fusion.1
  440.4 2.7 pad_maximum_fusion
  443.1 2.0 fusion.135
  445.4 4.1 fusion.122
  449.6 1.8 fusion.1
  456.3 3.7 all-to-all-start.2
  460.0 1.8 reshape.414
  462.7 2.5 convolution_convert_fusion.4
  465.4 3.4 all-to-all-done.2
  468.8 2.3 reshape.428
  473.5 2.0 fusion.23
  485.0 2.2 reshape.423
  487.2 2.8 fusion.18
  490.0 1.8 reshape.415
  491.8 1.8 slice_multiply_fusion.2
  496.2 2.3 fusion.123
  498.5 2.4 reshape.416
  500.8 2.2 copy.118
  503.1 2.6 reshape.417
  505.7 21.9 %all_to_all.20 = bf16[32,3,24,128]{3,2,1,0:T(8,128)(2,1)S(1)} all-to-all(bf16[32,3,24,128]{3,2,1,0:T(8,128)(2,1)S(1)} %reshape.417), channel_id=1, replica_groups=mesh['blk'=8,'chan'=4] {'blk','chan'}, dimensions={0} | all-to-all | bytes 1179648 | tf_op jit(solution)/shard_map/all_to_all | solution.py:143
  527.6 2.9 convolution_convert_fusion.2
  531.7 3.7 convolution_convert_fusion.1
  536.4 5.2 convolution_convert_fusion
  543.9 4.6 fusion.13
  549.8 2.3 stack.126
  557.3 2.0 fusion.5
  559.4 3.5 multiply_reduce_fusion.3
  568.5 2.3 fusion.34
  571.0 3.8 fusion.2
  575.5 1.7 fusion.83
  577.2 2.9 fusion.35
  581.1 39.5 %all-reduce.37 = (f32[4,768]{1,0:T(4,128)S(1)}, f32[100,64]{0,1:T(8,128)S(1)}) all-reduce(f32[4,768]{1,0:T(4,128)S(1)} %pad_maximum_fusion.31, f32[100,64]{0,1:T(8,128)S(1)} %concatenate.140), channel_id=6, replica_groups=mesh['blk'=8,'chan'=4] {'blk','chan'}, use_global_device_ids=true, to_apply=%region_16.17.clone | all-reduce | flops 9472 | bytes 75776
  625.7 46.4 %reduce-scatter.6.cloned.1.call-done = bf16[72,768]{1,0:T(8,128)(2,1)} async-done(((bf16[2304,768]{1,0:T(8,128)(2,1)}), bf16[72,768]{1,0:T(8,128)(2,1)}) %reduce-scatter.6.cloned.1.call-update) | async-done | bytes 110608 | tf_op jit(solution)/shard_map/reduce_scatter | solution.py:343
  673.7 109.9 %reduce-scatter.10.cloned.1.call-done = bf16[96,768]{1,0:T(8,128)(2,1)} async-done(((bf16[3072,768]{1,0:T(8,128)(2,1)}), bf16[96,768]{1,0:T(8,128)(2,1)}) %reduce-scatter.10.cloned.1.call-update) | async-done | bytes 147472 | tf_op jit(solution)/shard_map/reduce_scatter | solution.py:343
  785.3 110.7 %reduce-scatter.12.cloned.1.call-done = bf16[96,768]{1,0:T(8,128)(2,1)} async-done(((bf16[3072,768]{1,0:T(8,128)(2,1)}), bf16[96,768]{1,0:T(8,128)(2,1)}) %reduce-scatter.12.cloned.1.call-update) | async-done | bytes 147472 | tf_op jit(solution)/shard_map/reduce_scatter | solution.py:343
  (579 shorter events, 111.2 us)
Async XLA Ops:
  7.2 54.9 %copy-start = (bf16[64,64]{1,0:T(8,128)(2,1)S(1)}, bf16[64,64]{1,0:T(8,128)(2,1)}, u32[]{:S(2)}) copy-start(bf16[64,64]{1,0:T(8,128)(2,1)} %param.36) | copy-start | bytes 24580
  7.2 62.7 %collective-permute-start = (bf16[1,72,768]{2,1,0:T(8,128)(2,1)}, bf16[1,72,768]{2,1,0:T(8,128)(2,1)S(1)}, u32[]{:S(2)}, u32[]{:S(2)}) collective-permute-start(bf16[1,72,768]{2,1,0:T(8,128)(2,1)} %bitcast.404), channel_id=1, source_target_pairs={{0,1},{1,0},{2,3},{3,2},{4,5},{5,4},{6,7},{7,6},{8,9},{9,8},{10,11... | collective-permute-start | bytes 331784 | tf_op jit(solution)/shard_map/ppermute | solution.py:27
  7.7 62.4 %collective-permute-start.5 = (bf16[1,24,768]{2,1,0:T(8,128)(2,1)}, bf16[1,24,768]{2,1,0:T(8,128)(2,1)S(1)}, u32[]{:S(2)}, u32[]{:S(2)}) collective-permute-start(bf16[1,24,768]{2,1,0:T(8,128)(2,1)} %bitcast.406), channel_id=1, source_target_pairs={{0,1},{1,0},{2,3},{3,2},{4,5},{5,4},{6,7},{7,6},{8,9},{9,8},{10,11... | collective-permute-start | bytes 110600 | tf_op jit(solution)/shard_map/ppermute | solution.py:27
  7.8 88.3 %collective-permute-start.15 = (bf16[1,96,768]{2,1,0:T(8,128)(2,1)}, bf16[1,96,768]{2,1,0:T(8,128)(2,1)S(1)}, u32[]{:S(2)}, u32[]{:S(2)}) collective-permute-start(bf16[1,96,768]{2,1,0:T(8,128)(2,1)} %bitcast.402), channel_id=1, source_target_pairs={{0,1},{1,0},{2,3},{3,2},{4,5},{5,4},{6,7},{7,6},{8,9},{9,8},{10,11... | collective-permute-start | bytes 442376 | tf_op jit(solution)/shard_map/ppermute | solution.py:27
  8.2 87.8 %collective-permute-start.10 = (bf16[1,96,768]{2,1,0:T(8,128)(2,1)}, bf16[1,96,768]{2,1,0:T(8,128)(2,1)S(1)}, u32[]{:S(2)}, u32[]{:S(2)}) collective-permute-start(bf16[1,96,768]{2,1,0:T(8,128)(2,1)} %bitcast.403), channel_id=1, source_target_pairs={{0,1},{1,0},{2,3},{3,2},{4,5},{5,4},{6,7},{7,6},{8,9},{9,8},{10,11... | collective-permute-start | bytes 442376 | tf_op jit(solution)/shard_map/ppermute | solution.py:27
  8.3 59.7 %copy-start.128 = (pred[256]{0:T(512)(128)(4,1)}, pred[256]{0:T(512)(128)(4,1)S(1)}, u32[]{:S(2)}) copy-start(pred[256]{0:T(512)(128)(4,1)S(1)} %get-tuple-element.278) | copy-start | bytes 772
  8.3 55.9 %copy-start.138 = (bf16[64,24]{0,1:T(8,128)(2,1)S(1)}, bf16[64,24]{0,1:T(8,128)(2,1)}, u32[]{:S(2)}) copy-start(bf16[64,24]{0,1:T(8,128)(2,1)} %param.33) | copy-start | bytes 9220
  9.3 57.0 %copy-start.126 = (f32[1,2048]{1,0:T(1,128)}, f32[1,2048]{1,0:T(1,128)S(1)}, u32[]{:S(2)}) copy-start(f32[1,2048]{1,0:T(1,128)S(1)} %convert_multiply_fusion.1) | copy-start | bytes 24580
  10.0 58.1 %copy-start.152 = (f32[256]{0:T(256)}, f32[256]{0:T(256)S(1)}, u32[]{:S(2)}) copy-start(f32[256]{0:T(256)S(1)} %get-tuple-element.281) | copy-start | bytes 3076
  55.9 12.6 %copy-start.150 = (f32[2,64]{1,0:T(2,128)}, f32[2,64]{1,0:T(2,128)S(1)}, u32[]{:S(2)}) copy-start(f32[2,64]{1,0:T(2,128)S(1)} %broadcast_multiply_fusion) | copy-start | bytes 1540
  57.0 11.5 %copy-start.162 = (f32[2,64]{1,0:T(2,128)}, f32[2,64]{1,0:T(2,128)S(1)}, u32[]{:S(2)}) copy-start(f32[2,64]{1,0:T(2,128)S(1)} %add_rsqrt_fusion) | copy-start | bytes 1540
  59.0 7.4 copy-start.136
  59.7 6.7 copy-start.159
  62.1 5.9 copy-start.23
  67.4 283.7 %copy-start.8 = (f32[256,256]{1,0:T(8,128)}, f32[256,256]{1,0:T(8,128)S(1)}, u32[]{:S(2)}) copy-start(f32[256,256]{1,0:T(8,128)S(1)} %negate_select_fusion.2) | copy-start | bytes 786436
  69.9 9.2 %copy-start.169 = (bf16[3,24]{1,0:T(4,128)(2,1)S(1)}, bf16[3,24]{1,0:T(4,128)(2,1)}, u32[]{:S(2)}) copy-start(bf16[3,24]{1,0:T(4,128)(2,1)} %param.31) | copy-start | bytes 436
  70.0 8.3 collective-permute-start.1
  70.1 23.0 %copy-start.170 = (bf16[24]{0:T(256)(128)(2,1)S(1)}, bf16[24]{0:T(256)(128)(2,1)}, u32[]{:S(2)}) copy-start(bf16[24]{0:T(256)(128)(2,1)} %param.32) | copy-start | bytes 148
  70.2 23.5 %collective-permute-start.6 = (bf16[2,24,768]{2,1,0:T(8,128)(2,1)S(1)}, bf16[2,24,768]{2,1,0:T(8,128)(2,1)S(1)}, u32[]{:S(2)}, u32[]{:S(2)}) collective-permute-start(bf16[2,24,768]{2,1,0:T(8,128)(2,1)S(1)} %pad_maximum_fusion.24), channel_id=1, source_target_pairs={{0,2},{1,3},{2,0},{3,1},{4,6},{5,7},{6,4},{7,5},{8,10},{9,11},{10,... | collective-permute-start | bytes 221192 | tf_op jit(solution)/shard_map/ppermute | solution.py:27
  78.4 15.3 %collective-permute-start.2 = (bf16[4,72,768]{2,1,0:T(8,128)(2,1)S(1)}, bf16[4,72,768]{2,1,0:T(8,128)(2,1)S(1)}, u32[]{:S(2)}, u32[]{:S(2)}) collective-permute-start(bf16[4,72,768]{2,1,0:T(8,128)(2,1)S(1)} %pad_maximum_fusion.15), channel_id=1, source_target_pairs={{0,4},{1,5},{2,6},{3,7},{4,0},{5,1},{6,2},{7,3},{8,12},{9,13},{10,... | collective-permute-start | bytes 1327112 | tf_op jit(solution)/shard_map/ppermute | solution.py:27
  93.9 23.0 %collective-permute-start.3 = (bf16[8,72,768]{2,1,0:T(8,128)(2,1)S(1)}, bf16[8,72,768]{2,1,0:T(8,128)(2,1)S(1)}, u32[]{:S(2)}, u32[]{:S(2)}) collective-permute-start(bf16[8,72,768]{2,1,0:T(8,128)(2,1)S(1)} %pad_maximum_fusion.10), channel_id=1, source_target_pairs={{0,8},{1,9},{2,10},{3,11},{4,12},{5,13},{6,14},{7,15},{8,0},{9,1},... | collective-permute-start | bytes 2654216 | tf_op jit(solution)/shard_map/ppermute | solution.py:27
  94.0 5.2 collective-permute-start.7
  96.2 21.1 %collective-permute-start.16 = (bf16[2,96,768]{2,1,0:T(8,128)(2,1)S(1)}, bf16[2,96,768]{2,1,0:T(8,128)(2,1)S(1)}, u32[]{:S(2)}, u32[]{:S(2)}) collective-permute-start(bf16[2,96,768]{2,1,0:T(8,128)(2,1)S(1)} %pad_maximum_fusion.19), channel_id=1, source_target_pairs={{0,2},{1,3},{2,0},{3,1},{4,6},{5,7},{6,4},{7,5},{8,10},{9,11},{10,... | collective-permute-start | bytes 884744 | tf_op jit(solution)/shard_map/ppermute | solution.py:27
  96.3 23.0 %collective-permute-start.11 = (bf16[2,96,768]{2,1,0:T(8,128)(2,1)S(1)}, bf16[2,96,768]{2,1,0:T(8,128)(2,1)S(1)}, u32[]{:S(2)}, u32[]{:S(2)}) collective-permute-start(bf16[2,96,768]{2,1,0:T(8,128)(2,1)S(1)} %pad_maximum_fusion.18), channel_id=1, source_target_pairs={{0,2},{1,3},{2,0},{3,1},{4,6},{5,7},{6,4},{7,5},{8,10},{9,11},{10,... | collective-permute-start | bytes 884744 | tf_op jit(solution)/shard_map/ppermute | solution.py:27
  99.3 22.9 %collective-permute-start.8 = (bf16[8,24,768]{2,1,0:T(8,128)(2,1)S(1)}, bf16[8,24,768]{2,1,0:T(8,128)(2,1)S(1)}, u32[]{:S(2)}, u32[]{:S(2)}) collective-permute-start(bf16[8,24,768]{2,1,0:T(8,128)(2,1)S(1)} %pad_maximum_fusion.17), channel_id=1, source_target_pairs={{0,8},{1,9},{2,10},{3,11},{4,12},{5,13},{6,14},{7,15},{8,0},{9,1},... | collective-permute-start | bytes 884744 | tf_op jit(solution)/shard_map/ppermute | solution.py:27
  117.2 89.1 %collective-permute-start.4 = (bf16[16,72,768]{2,1,0:T(8,128)(2,1)S(1)}, bf16[16,72,768]{2,1,0:T(8,128)(2,1)S(1)}, u32[]{:S(2)}, u32[]{:S(2)}) collective-permute-start(bf16[16,72,768]{2,1,0:T(8,128)(2,1)S(1)} %pad_maximum_fusion.5), channel_id=1, source_target_pairs={{0,16},{1,17},{2,18},{3,19},{4,20},{5,21},{6,22},{7,23},{8,24},{9,... | collective-permute-start | bytes 5308424 | tf_op jit(solution)/shard_map/ppermute | solution.py:27
  117.4 16.3 %collective-permute-start.17 = (bf16[4,96,768]{2,1,0:T(8,128)(2,1)S(1)}, bf16[4,96,768]{2,1,0:T(8,128)(2,1)S(1)}, u32[]{:S(2)}, u32[]{:S(2)}) collective-permute-start(bf16[4,96,768]{2,1,0:T(8,128)(2,1)S(1)} %pad_maximum_fusion.13), channel_id=1, source_target_pairs={{0,4},{1,5},{2,6},{3,7},{4,0},{5,1},{6,2},{7,3},{8,12},{9,13},{10,... | collective-permute-start | bytes 1769480 | tf_op jit(solution)/shard_map/ppermute | solution.py:27
  119.4 21.4 %collective-permute-start.12 = (bf16[4,96,768]{2,1,0:T(8,128)(2,1)S(1)}, bf16[4,96,768]{2,1,0:T(8,128)(2,1)S(1)}, u32[]{:S(2)}, u32[]{:S(2)}) collective-permute-start(bf16[4,96,768]{2,1,0:T(8,128)(2,1)S(1)} %pad_maximum_fusion.12), channel_id=1, source_target_pairs={{0,4},{1,5},{2,6},{3,7},{4,0},{5,1},{6,2},{7,3},{8,12},{9,13},{10,... | collective-permute-start | bytes 1769480 | tf_op jit(solution)/shard_map/ppermute | solution.py:27
  123.1 94.5 %collective-permute-start.9 = (bf16[16,24,768]{2,1,0:T(8,128)(2,1)}, bf16[16,24,768]{2,1,0:T(8,128)(2,1)}, u32[]{:S(2)}, u32[]{:S(2)}) collective-permute-start(bf16[16,24,768]{2,1,0:T(8,128)(2,1)} %pad_maximum_fusion.11), channel_id=1, source_target_pairs={{0,16},{1,17},{2,18},{3,19},{4,20},{5,21},{6,22},{7,23},{8,24},{9,... | collective-permute-start | bytes 1769480 | tf_op jit(solution)/shard_map/ppermute | solution.py:27
  134.9 85.0 %collective-permute-start.18 = (bf16[8,96,768]{2,1,0:T(8,128)(2,1)}, bf16[8,96,768]{2,1,0:T(8,128)(2,1)}, u32[]{:S(2)}, u32[]{:S(2)}) collective-permute-start(bf16[8,96,768]{2,1,0:T(8,128)(2,1)} %pad_maximum_fusion.8), channel_id=1, source_target_pairs={{0,8},{1,9},{2,10},{3,11},{4,12},{5,13},{6,14},{7,15},{8,0},{9,1},... | collective-permute-start | bytes 3538952 | tf_op jit(solution)/shard_map/ppermute | solution.py:27
  142.1 91.1 %collective-permute-start.13 = (bf16[8,96,768]{2,1,0:T(8,128)(2,1)}, bf16[8,96,768]{2,1,0:T(8,128)(2,1)}, u32[]{:S(2)}, u32[]{:S(2)}) collective-permute-start(bf16[8,96,768]{2,1,0:T(8,128)(2,1)} %pad_maximum_fusion.7), channel_id=1, source_target_pairs={{0,8},{1,9},{2,10},{3,11},{4,12},{5,13},{6,14},{7,15},{8,0},{9,1},... | collective-permute-start | bytes 3538952 | tf_op jit(solution)/shard_map/ppermute | solution.py:27
  209.7 122.9 %all-to-all-start = ((bf16[32,3,24,128]{3,2,1,0:T(8,128)(2,1)}), bf16[32,3,24,128]{3,2,1,0:T(8,128)(2,1)}, u32[]{:S(2)}, u32[]{:S(2)}) async-start(bf16[32,3,24,128]{3,2,1,0:T(8,128)(2,1)} %bitcast.321), calls=%async_computation | async-start | bytes 1179648 | tf_op jit(solution)/shard_map/all_to_all | solution.py:143
  223.6 161.7 %collective-permute-start.19 = (bf16[16,96,768]{2,1,0:T(8,128)(2,1)}, bf16[16,96,768]{2,1,0:T(8,128)(2,1)}, u32[]{:S(2)}, u32[]{:S(2)}) collective-permute-start(bf16[16,96,768]{2,1,0:T(8,128)(2,1)} %pad_maximum_fusion.4), channel_id=1, source_target_pairs={{0,16},{1,17},{2,18},{3,19},{4,20},{5,21},{6,22},{7,23},{8,24},{9,... | collective-permute-start | bytes 7077896 | tf_op jit(solution)/shard_map/ppermute | solution.py:27
  236.7 199.1 %collective-permute-start.14 = (bf16[16,96,768]{2,1,0:T(8,128)(2,1)}, bf16[16,96,768]{2,1,0:T(8,128)(2,1)}, u32[]{:S(2)}, u32[]{:S(2)}) collective-permute-start(bf16[16,96,768]{2,1,0:T(8,128)(2,1)} %pad_maximum_fusion.3), channel_id=1, source_target_pairs={{0,16},{1,17},{2,18},{3,19},{4,20},{5,21},{6,22},{7,23},{8,24},{9,... | collective-permute-start | bytes 7077896 | tf_op jit(solution)/shard_map/ppermute | solution.py:27
  355.1 30.2 %copy-start.14 = (bf16[8,96,768]{2,1,0:T(8,128)(2,1)S(1)}, bf16[8,96,768]{2,1,0:T(8,128)(2,1)}, u32[]{:S(2)}) copy-start(bf16[8,96,768]{2,1,0:T(8,128)(2,1)} %copy-done.13) | copy-start | bytes 3538948
  358.1 84.9 %all-to-all-start.1 = ((bf16[32,1,24,128]{3,2,1,0:T(8,128)(2,1)}), bf16[32,1,24,128]{3,2,1,0:T(8,128)(2,1)}, u32[]{:S(2)}, u32[]{:S(2)}) async-start(bf16[32,1,24,128]{3,2,1,0:T(8,128)(2,1)} %bitcast.331), calls=%async_computation.1 | async-start | bytes 393216 | tf_op jit(solution)/shard_map/all_to_all | solution.py:143
  361.8 74.0 %copy-start.17 = (bf16[8,96,768]{2,1,0:T(8,128)(2,1)S(1)}, bf16[8,96,768]{2,1,0:T(8,128)(2,1)}, u32[]{:S(2)}) copy-start(bf16[8,96,768]{2,1,0:T(8,128)(2,1)} %copy-done.16) | copy-start | bytes 3538948
  361.8 74.0 %copy-start.19 = (bf16[8,96,768]{2,1,0:T(8,128)(2,1)S(1)}, bf16[8,96,768]{2,1,0:T(8,128)(2,1)}, u32[]{:S(2)}) copy-start(bf16[8,96,768]{2,1,0:T(8,128)(2,1)} %copy-done.18) | copy-start | bytes 3538948
  445.1 8.7 copy-start.147
  445.3 8.5 copy-start.154
  445.4 6.0 slice-start
  455.1 7.7 copy-start.31
  455.1 6.8 copy-start.44
  456.3 12.6 %all-to-all-start.2 = ((bf16[32,1,24,128]{3,2,1,0:T(8,128)(2,1)}), bf16[32,1,24,128]{3,2,1,0:T(8,128)(2,1)}, u32[]{:S(2)}, u32[]{:S(2)}) async-start(bf16[32,1,24,128]{3,2,1,0:T(8,128)(2,1)} %bitcast.330), calls=%async_computation.2 | async-start | bytes 393216 | tf_op jit(solution)/shard_map/all_to_all | solution.py:143
  460.0 164.4 %reduce-scatter.8.cloned.1.call-start = ((), (), s32[]{:S(2)}) async-start(), calls=%async_computation.9 | async-start | bytes 1216512 | tf_op jit(solution)/shard_map/reduce_scatter | solution.py:343
  465.2 206.9 %reduce-scatter.6.cloned.1.call-start = ((), (), s32[]{:S(2)}) async-start(), calls=%async_computation.8 | async-start | bytes 3649536 | tf_op jit(solution)/shard_map/reduce_scatter | solution.py:343
  485.0 6.8 copy-start.168
  505.6 22.0 %copy-start.52 = (bf16[2,1,64,768]{3,2,1,0:T(8,128)(2,1)S(1)}, bf16[2,1,64,768]{3,2,1,0:T(8,128)(2,1)}, u32[]{:S(2)}) copy-start(bf16[2,1,64,768]{3,2,1,0:T(8,128)(2,1)} %add_convert_fusion.3) | copy-start | bytes 589828
  530.6 253.1 %reduce-scatter.10.cloned.1.call-start = ((), (), s32[]{:S(2)}) async-start(), calls=%async_computation.10 | async-start | bytes 4866048 | tf_op jit(solution)/shard_map/reduce_scatter | solution.py:343
  535.5 360.5 %reduce-scatter.12.cloned.1.call-start = ((), (), s32[]{:S(2)}) async-start(), calls=%async_computation.11 | async-start | bytes 4866048 | tf_op jit(solution)/shard_map/reduce_scatter | solution.py:343
  543.9 4.6 copy-start.34
  548.5 4.7 copy-start.11
  549.8 4.6 copy-start.130
  557.3 5.9 copy-start.46
  559.4 5.3 copy-start.47
  566.3 4.6 copy-start.4
  571.0 4.5 copy-start.22
  571.0 6.3 copy-start.161
  571.0 9.1 %copy-start.2 = (bf16[32,72,768]{2,1,0:T(8,128)(2,1)S(1)}, bf16[32,72,768]{2,1,0:T(8,128)(2,1)}, u32[]{:S(2)}) copy-start(bf16[32,72,768]{2,1,0:T(8,128)(2,1)} %copy-done.1) | copy-start | bytes 10616836
  574.9 5.3 copy-start.28
  574.9 5.3 copy-start.39
  574.9 5.3 copy-start.165
  574.9 5.3 copy-start.166
  580.2 43.3 %copy-start.32 = (f32[128,768]{1,0:T(8,128)S(1)}, f32[128,768]{1,0:T(8,128)}, u32[]{:S(2)}) copy-start(f32[128,768]{1,0:T(8,128)} %copy-done.31) | copy-start | bytes 1179652
  (136 other events, 225.7 us)
Sparse Core Ops, SparseCore 0:
  465.9 98.4 reduce-scatter.7
  569.8 102.2 reduce-scatter.5
  677.6 105.9 reduce-scatter.9
  789.9 106.0 reduce-scatter.11
